TPU v7x, 256 devices: a whole 4x4x8 slice. The times are simulated.
256 devices in a mesh: dp: 2 (over z_lo), seq: 32 (over y, x, core), head: 4 (over z_hi).
Axes of the slice: x: 4, y: 4, z: 8 (z_hi: 4, z_lo: 2; z = z_hi * 2 + z_lo), core: 2. Of those that a mesh axis runs over, the one named last changes fastest.
Arguments:
- x_in: bfloat16 [2, 24576, 4096], P('dp', 'seq', 'head'), may hold values from -6 to 6
- b_in: bfloat16 [2, 24576, 1024], P('dp', 'seq', 'head'), may hold values from -6 to 6
- c_in: bfloat16 [2, 24576, 1024], P('dp', 'seq', 'head'), may hold values from -6 to 6
- z_in: bfloat16 [2, 24576, 4096], P('dp', 'seq', 'head'), may hold values from -24 to 24
- dt_in: float32 [2, 64, 24576], P('dp', 'head', 'seq'), may hold values from -10 to 4.5
- a_log: float32 [64], P('head'), may hold values from -2.3 to 0.58
- skip_gain: float32 [64], P('head'), may hold values from 0.5 to 1.5
- norm_gain: float32 [4096], P('head'), may hold values from 0.5 to 1.5
- conv_x: float32 [4, 4096], P(None, 'head'), may hold values from -3 to 3
- conv_b: float32 [4, 1024], P(None, 'head'), may hold values from -3 to 3
- conv_c: float32 [4, 1024], P(None, 'head'), may hold values from -3 to 3
- init_state: float32 [2, 64, 64, 128], P('dp', 'head'), may hold values from -0.5 to 0.5
- out_weight: bfloat16 [4096, 8192], P(('dp', 'seq'), 'head'), may hold values from -0.09375 to 0.09375
Outputs:
- mixed: bfloat16 [2, 24576, 8192], P('dp', 'seq', 'head')
All inputs are finite; a program needn't handle non-finite values.
Results may differ from a plain program's by a relative error of at most 0.0058.
Values may be sent and summed in bfloat16 or wider, within the bound.
No kernel may reach another device: no remote copies, remote signals or barrier semaphores. Data moves between devices by JAX's collectives and lax.ppermute only.
A program may use at most 128 MiB of HBM per device.

v0:
```python
import jax
import jax.numpy as jnp
from jax import lax
from jax.sharding import PartitionSpec as P

HEAD_SIZE = 64
STATE = 128
BLOCK_LEN = 256
TAPS = 4
EPSILON = 1e-05


def from_behind(block, axis, distance):
    devices = range(lax.axis_size(axis))
    route = [(i - distance, i) for i in devices if i - distance in devices]
    return lax.ppermute(block, axis, route)


def entering(value, axis, join, neutral):
    count, mine = (lax.axis_size(axis), lax.axis_index(axis))
    pieces = jax.tree.map(lambda part: lax.all_gather(part, axis), value)
    subtotal = jax.tree.map(
        lambda part, zero: jnp.full_like(part, 0) + jnp.asarray(zero, part.dtype), value, neutral
    )

    def step(position, subtotal):
        longer = join(subtotal, jax.tree.map(lambda part: part[position], pieces))
        return jax.tree.map(lambda new, old: jnp.where(position < mine, new, old), longer, subtotal)

    return lax.fori_loop(0, count - 1, step, subtotal)


def causal_conv(signal, before, weight):
    joined = jnp.concatenate([before, signal], axis=1).astype(jnp.float32)
    length = signal.shape[1]
    tap_count = weight.shape[0]
    accum_total = weight[0] * joined[:, 0:length]
    for offset in range(1, tap_count):
        accum_total = accum_total + weight[offset] * joined[:, offset : offset + length]
    return jax.nn.silu(accum_total).astype(jnp.bfloat16)


def combine_states(first_pair, second_pair):
    return (
        first_pair[0] * second_pair[0],
        second_pair[0][..., None, None] * first_pair[1] + second_pair[1],
    )


def local(
    x_in,
    b_in,
    c_in,
    z_in,
    dt_in,
    a_log,
    skip_gain,
    norm_gain,
    conv_x,
    conv_b,
    conv_c,
    init_state,
    out_weight,
):
    highest = lax.Precision.HIGHEST
    roll_count, tok_count, wide_x = x_in.shape
    wide_b = b_in.shape[2]
    head_count = dt_in.shape[1]
    group_count = wide_b // STATE
    per_group = head_count // group_count
    block_count = tok_count // BLOCK_LEN
    rim_width = TAPS - 1
    edge_rows = jnp.concatenate(
        [
            x_in[:, tok_count - rim_width :],
            b_in[:, tok_count - rim_width :],
            c_in[:, tok_count - rim_width :],
        ],
        axis=2,
    )
    before = from_behind(edge_rows, "seq", 1)
    x_conv = causal_conv(x_in, before[:, :, :wide_x], conv_x)
    b_conv = causal_conv(b_in, before[:, :, wide_x : wide_x + wide_b], conv_b)
    c_conv = causal_conv(c_in, before[:, :, wide_x + wide_b :], conv_c)
    grouped = (roll_count, group_count, per_group, block_count, BLOCK_LEN)
    step_flat = jax.nn.softplus(dt_in)
    decay_rate = -jnp.exp(a_log)
    cum_decay = jnp.cumsum((step_flat * decay_rate[None, :, None]).reshape(grouped), axis=-1)
    step_size = step_flat.reshape(grouped)
    x_shaped = x_conv.reshape(roll_count, block_count, BLOCK_LEN, group_count, per_group, HEAD_SIZE)
    b_shaped = b_conv.reshape(roll_count, block_count, BLOCK_LEN, group_count, STATE)
    c_shaped = c_conv.reshape(roll_count, block_count, BLOCK_LEN, group_count, STATE)
    scores = jnp.einsum(
        "rcqgn,rcsgn->rgcqs", c_shaped, b_shaped, preferred_element_type=jnp.float32
    )
    query_pos = lax.broadcasted_iota(jnp.int32, (BLOCK_LEN, BLOCK_LEN), 0)
    key_pos = lax.broadcasted_iota(jnp.int32, (BLOCK_LEN, BLOCK_LEN), 1)
    causal = query_pos >= key_pos
    spread = cum_decay[..., :, None] - cum_decay[..., None, :]
    decay_mat = jnp.where(causal, jnp.exp(jnp.minimum(spread, 0.0)), jnp.float32(0.0))
    mixing = (scores[:, :, None] * decay_mat * step_size[..., None, :]).astype(jnp.bfloat16)
    intra_out = jnp.einsum(
        "rgkcqs,rcsgkp->rcqgkp", mixing, x_shaped, preferred_element_type=jnp.float32
    )
    last_decay = cum_decay[..., -1:]
    weights_in = jnp.exp(last_decay - cum_decay) * step_size
    weighted = (
        jnp.transpose(weights_in, (0, 3, 4, 1, 2))[..., None] * x_shaped.astype(jnp.float32)
    ).astype(jnp.bfloat16)
    block_states = jnp.einsum(
        "rcsgkp,rcsgn->rgkcpn", weighted, b_shaped, preferred_element_type=jnp.float32
    )
    block_decay = jnp.exp(last_decay[..., 0])
    running = jnp.zeros((roll_count, group_count, per_group, HEAD_SIZE, STATE), jnp.float32)
    carried = jnp.ones((roll_count, group_count, per_group), jnp.float32)
    starts = []
    factors = []
    for block_index in range(block_count):
        starts.append(running)
        factors.append(carried)
        running = (
            block_decay[..., block_index, None, None] * running + block_states[:, :, :, block_index]
        )
        carried = carried * block_decay[..., block_index]
    prefix_decay, prefix_state = entering(
        (carried, running), "seq", combine_states, (jnp.ones_like(carried), jnp.zeros_like(running))
    )
    incoming = prefix_state + prefix_decay[..., None, None] * init_state.reshape(
        roll_count, group_count, per_group, HEAD_SIZE, STATE
    )
    start_states = jnp.stack(
        [
            factors[block_index][..., None, None] * incoming + starts[block_index]
            for block_index in range(block_count)
        ],
        axis=3,
    )
    c_float = c_shaped.astype(jnp.float32)
    inter_out = jnp.einsum("rcqgn,rgkcpn->rcqgkp", c_float, start_states, precision=highest)
    inter_out = inter_out * jnp.transpose(jnp.exp(cum_decay), (0, 3, 4, 1, 2))[..., None]
    skip_shaped = skip_gain.reshape(group_count, per_group)[:, :, None]
    ssm_out = (intra_out + inter_out + skip_shaped * x_shaped.astype(jnp.float32)).reshape(
        roll_count, tok_count, group_count, per_group * HEAD_SIZE
    )
    gate_act = jax.nn.silu(z_in.astype(jnp.float32)).reshape(
        roll_count, tok_count, group_count, per_group * HEAD_SIZE
    )
    gated_out = ssm_out * gate_act
    mean_sq = jnp.mean(gated_out * gated_out, axis=-1, keepdims=True)
    normed = (
        gated_out
        * lax.rsqrt(mean_sq + EPSILON)
        * norm_gain.reshape(group_count, per_group * HEAD_SIZE)
    )
    normed = normed.astype(jnp.bfloat16).reshape(roll_count * tok_count, wide_x)
    wide_all = lax.all_gather(normed, "head", axis=1, tiled=True)
    full_weight = lax.all_gather(out_weight, ("dp", "seq"), axis=0, tiled=True)
    mixed_terms = jnp.dot(wide_all, full_weight, preferred_element_type=jnp.float32)
    return mixed_terms.astype(jnp.bfloat16).reshape(roll_count, tok_count, -1)


def solution(mesh):
    in_specs = (
        P("dp", "seq", "head"),
        P("dp", "seq", "head"),
        P("dp", "seq", "head"),
        P("dp", "seq", "head"),
        P("dp", "head", "seq"),
        P("head"),
        P("head"),
        P("head"),
        P(None, "head"),
        P(None, "head"),
        P(None, "head"),
        P("dp", "head", None, None),
        P(("dp", "seq"), "head"),
    )
    out_specs = P("dp", "seq", "head")
    return jax.shard_map(local, mesh=mesh, in_specs=in_specs, out_specs=out_specs, check_vma=False)
```

profile of v0, /device:TPU:65, one launch (start us, length us, event | category | flops | bytes accessed | tf_op | source)
XLA Modules:
  0.0 390.5 jit_solution(8210310024297503800)
XLA Ops:
  9.6 3.7 collective-permute-start
  14.9 3.4 reduce-window.6
  22.2 1.7 copy.154
  26.1 3.5 multiply_convert_fusion.3
  29.7 2.1 reshape.545
  33.5 2.6 multiply_convert_fusion.2
  38.9 2.6 copy.182
  41.5 3.9 convert_multiply_fusion
  45.5 5.9 %reshape.560 = f32[1,3,256,2,8,64]{2,1,5,4,3,0:T(4,128)} reshape(f32[1,768,1024]{1,2,0:T(8,128)} %convert_multiply_fusion) | data formatting | bytes 6291456 | tf_op jit(solution)/shard_map/reshape | solution.py:145
  52.1 25.1 %all-gather = f32[32,2,8,1]{2,1,3,0:T(2,128)} all-gather(f32[1,2,8,1]{2,1,3,0:T(2,128)S(1)} %copy-done.18), channel_id=2, replica_groups=mesh['dp'=2,'seq'=32,'head'=4] {'seq'}, dimensions={0}, use_global_device_ids=true | all-gather | bytes 2112 | tf_op jit(solution)/shard_map/all_gather | solution.py:21
  78.5 5.7 %reshape.562 = f32[1,3,256,2,8,64]{2,1,5,4,3,0:T(4,128)} reshape(bf16[1,768,1024]{1,2,0:T(8,128)(2,1)} %copy-done.1) | data formatting | bytes 4718592 | tf_op jit(solution)/shard_map/convert_element_type | solution.py:108
  84.4 1.2 multiply_convert_fusion.5
  85.7 1.6 fusion.44
  87.2 7.5 %fusion.1 = f32[3,2,8,64,256]{4,3,2,1,0:T(8,128)} fusion(f32[2,3,256,256]{3,2,0,1:T(8,128)} %fusion.44, pred[256,256]{1,0:T(8,128)(4,1)S(1)} %iota_compare_fusion, bf16[3,256,2,8,64]{1,0,4,3,2:T(4,128)(2,1)} %reshape.545, f32[2,8,3,256]{3,1,2,0:T(8,128)S(1)} %bitcast.161, f32[2,8,3,256]{3,1,2,0:T(8,128)S(1)} %copy-done.8), kind=kOutput, calls=%fused_computation.5 | convolution fusion | flops 421527552 | bytes 6455296 | tf_op jit(solution)/shard_map/rgkcqs,rcsgkp->rcqgkp/dot_general | solution.py:102
  94.7 22.5 %all-gather.5.cloned.1.call-done = f32[32,1,2,8,64,128]{5,4,3,2,1,0:T(8,128)} async-done(((f32[1,1,2,8,64,128]{5,4,3,2,1,0:T(8,128)}), f32[32,1,2,8,64,128]{5,4,3,2,1,0:T(8,128)}) %all-gather.5.cloned.1.call-update) | async-done | bytes 16777232 | tf_op jit(solution)/shard_map/all_gather | solution.py:21
  117.3 78.2 %while.16 = (s32[]{:T(128)}, f32[1,2,8]{2,1,0:T(2,128)S(1)}, f32[1,2,8,64,128]{4,3,2,1,0:T(8,128)S(1)}, s32[]{:T(128)}, f32[32,1,2,8]{3,2,1,0:T(2,128)}, /*index...) while((s32[]{:T(128)}, f32[1,2,8]{2,1,0:T(2,128)S(1)}, ...), condition=%wide.region_3.4_spmd.clone, body=%wide.region_2.3_spmd.clone.sunk | while | flops 524340 | bytes 1573367 | solution.py:30
  118.0 1.2 fusion.59
  120.6 1.2 fusion.59
  123.1 1.2 fusion.59
  125.6 1.2 fusion.59
  128.1 1.2 fusion.59
  130.6 1.2 fusion.59
  135.6 1.2 fusion.59
  140.6 1.2 fusion.59
  143.1 1.2 fusion.59
  148.2 1.2 fusion.59
  150.7 1.2 fusion.59
  153.2 1.2 fusion.59
  155.8 1.2 fusion.59
  158.3 1.2 fusion.59
  160.8 1.2 fusion.59
  163.3 1.2 fusion.59
  165.8 1.2 fusion.59
  173.4 1.2 fusion.59
  175.9 1.2 fusion.59
  178.4 1.2 fusion.59
  180.9 1.2 fusion.59
  183.5 1.2 fusion.59
  186.0 1.2 fusion.59
  188.5 1.2 fusion.59
  191.1 1.2 fusion.59
  195.9 1.8 copy-done.2
  197.7 4.8 %fusion.19 = (f32[3,256,2]{1,2,0:T(2,128)S(1)}, f32[1,3,256,2,8,64]{2,5,4,3,1,0:T(8,128)S(1)}) fusion(f32[1,3,256,2,8,64]{2,1,5,4,3,0:T(4,128)S(1)} %copy-done.2, f32[1,3,256,2,8,64]{2,1,5,4,3,0:T(4,128)} %reshape.562, f32[2,8]{1,0:T(2,128)S(1)} %copy-done.15, f32[3,256,2,8]{1,3,2,0:T(8,128)S(1)} %bitcast.163, ...), kind=kOutput, calls=%fused_computation.35 | convolution fusion | flops 1214249472 | bytes 14604352 | tf_op jit(solution)/shard_map/rcqgn,rgkcpn->rcqgkp/dot_general | solution.py:139
  202.5 2.2 copy.181
  206.1 2.2 fusion.17
  208.4 34.6 %all-gather.9.cloned.1.call-done = bf16[4096,2048]{1,0:T(8,128)(2,1)} async-done(((bf16[64,2048]{1,0:T(8,128)(2,1)}), bf16[4096,2048]{1,0:T(8,128)(2,1)}) %all-gather.9.cloned.1.call-update) | async-done | bytes 16777232 | tf_op jit(solution)/shard_map/all_gather | solution.py:157
  243.0 121.2 %all-gather.7.cloned.1.call-done = bf16[768,4096]{0,1:T(8,128)(2,1)} async-done(((bf16[768,1024]{0,1:T(8,128)(2,1)}), bf16[768,4096]{0,1:T(8,128)(2,1)}) %all-gather.7.cloned.1.call-update) | async-done | bytes 6291472 | tf_op jit(solution)/shard_map/all_gather | solution.py:156
  364.2 19.8 %fusion.20 = bf16[1,768,2048]{2,1,0:T(8,128)(2,1)} fusion(bf16[768,4096]{0,1:T(8,128)(2,1)} %all-gather.7.cloned.1.call-done, bf16[4096,2048]{1,0:T(8,128)(2,1)} %all-gather.9.cloned.1.call-done), kind=kOutput, calls=%fused_computation.38 | convolution fusion | flops 12886474752 | bytes 26214400 | tf_op jit(solution)/shard_map/dot_general | solution.py:158
  (171 shorter events, 67.7 us)
Async XLA Ops:
  6.5 110.7 %all-gather.5.cloned.1.call-start = ((), (), s32[]{:S(2)}) async-start(), calls=%async_computation | async-start | bytes 17301504 | tf_op jit(solution)/shard_map/all_gather | solution.py:21
  9.6 14.8 %collective-permute-start = (bf16[1,3,1536]{1,2,0:T(8,128)(2,1)}, bf16[1,3,1536]{1,2,0:T(8,128)(2,1)}, u32[]{:S(2)}, u32[]{:S(2)}) collective-permute-start(bf16[1,3,1536]{1,2,0:T(8,128)(2,1)} %copy.153), channel_id=1, source_target_pairs={{0,4},{4,8},{8,12},{12,16},{16,20},{20,24},{24,28},{28,32},{32,36}... | collective-permute-start | bytes 27656 | tf_op jit(solution)/shard_map/ppermute | solution.py:16
  14.8 5.7 %copy-start.12 = (f32[4,1024]{1,0:T(4,128)S(1)}, f32[4,1024]{1,0:T(4,128)}, u32[]{:S(2)}) copy-start(f32[4,1024]{1,0:T(4,128)} %param.23) | copy-start | bytes 49156
  14.8 5.7 %copy-start.19 = (f32[4,256]{1,0:T(4,128)S(1)}, f32[4,256]{1,0:T(4,128)}, u32[]{:S(2)}) copy-start(f32[4,256]{1,0:T(4,128)} %param.24) | copy-start | bytes 12292
  18.6 3.1 copy-start.6
  21.1 15.5 %copy-start.13 = (f32[2,8]{1,0:T(2,128)}, f32[2,8]{1,0:T(2,128)S(1)}, u32[]{:S(2)}) copy-start(f32[2,8]{1,0:T(2,128)S(1)} %get-tuple-element.212) | copy-start | bytes 196
  22.2 14.4 %copy-start.10 = (f32[2,8]{1,0:T(2,128)}, f32[2,8]{1,0:T(2,128)S(1)}, u32[]{:S(2)}) copy-start(f32[2,8]{1,0:T(2,128)S(1)} %get-tuple-element.209) | copy-start | bytes 196
  29.6 3.7 copy-start.1
  29.7 3.1 copy-start.4
  37.7 205.3 %all-gather.9.cloned.1.call-start = ((), (), s32[]{:S(2)}) async-start(), calls=%async_computation.2 | async-start | bytes 17039360 | tf_op jit(solution)/shard_map/all_gather | solution.py:157
  38.5 325.7 %all-gather.7.cloned.1.call-start = ((), (), s32[]{:S(2)}) async-start(), calls=%async_computation.1 | async-start | bytes 7864320 | tf_op jit(solution)/shard_map/all_gather | solution.py:156
  45.4 6.0 %copy-start.22 = (f32[16]{0:T(128)S(1)}, f32[16]{0:T(128)}, u32[]{:S(2)}) copy-start(f32[16]{0:T(128)} %param.21) | copy-start | bytes 196
  45.4 6.6 %copy-start.18 = (f32[1,2,8,1]{2,1,3,0:T(2,128)S(1)}, f32[1,2,8,1]{2,1,3,0:T(2,128)}, u32[]{:S(2)}) copy-start(f32[1,2,8,1]{2,1,3,0:T(2,128)} %get-tuple-element.211) | copy-start | bytes 196
  45.4 31.7 %copy-start.20 = (f32[4,256]{1,0:T(4,128)S(1)}, f32[4,256]{1,0:T(4,128)}, u32[]{:S(2)}) copy-start(f32[4,256]{1,0:T(4,128)} %param.25) | copy-start | bytes 12292
  45.4 32.3 %copy-start.7 = (f32[2,8,3,2]{1,3,2,0:T(2,128)S(1)}, f32[2,8,3,2]{1,3,2,0:T(2,128)}, u32[]{:S(2)}) copy-start(f32[2,8,3,2]{1,3,2,0:T(2,128)} %copy-done.6) | copy-start | bytes 1156
  51.4 32.9 %copy-start.5 = (bf16[1,768,256]{2,1,0:T(8,128)(2,1)S(1)}, bf16[1,768,256]{2,1,0:T(8,128)(2,1)}, u32[]{:S(2)}) copy-start(bf16[1,768,256]{2,1,0:T(8,128)(2,1)} %param.17) | copy-start | bytes 1179652
  84.4 2.9 copy-start.8
  87.2 30.0 %copy-start.9 = (f32[1,2,8]{2,1,0:T(2,128)S(1)}, f32[1,2,8]{2,1,0:T(2,128)}, u32[]{:S(2)}) copy-start(f32[1,2,8]{2,1,0:T(2,128)} %custom-call) | copy-start | bytes 196
  117.3 78.2 %copy-start.3 = (f32[1,16,64,128]{3,2,1,0:T(8,128)S(1)}, f32[1,16,64,128]{3,2,1,0:T(8,128)}, u32[]{:S(2)}) copy-start(f32[1,16,64,128]{3,2,1,0:T(8,128)} %param.26) | copy-start | bytes 1572868
  117.3 78.2 %copy-start.11 = (f32[2,8]{1,0:T(2,128)S(1)}, f32[2,8]{1,0:T(2,128)}, u32[]{:S(2)}) copy-start(f32[2,8]{1,0:T(2,128)} %copy-done.10) | copy-start | bytes 196
  117.3 78.2 %copy-start.16 = (f32[2,8]{1,0:T(2,128)S(1)}, f32[2,8]{1,0:T(2,128)}, u32[]{:S(2)}) copy-start(f32[2,8]{1,0:T(2,128)} %get-tuple-element.213) | copy-start | bytes 196
  117.3 78.4 %copy-start.14 = (f32[2,8]{1,0:T(2,128)S(1)}, f32[2,8]{1,0:T(2,128)}, u32[]{:S(2)}) copy-start(f32[2,8]{1,0:T(2,128)} %copy-done.13) | copy-start | bytes 196
  117.3 78.4 %copy-start.17 = (f32[2,8]{1,0:T(2,128)S(1)}, f32[2,8]{1,0:T(2,128)}, u32[]{:S(2)}) copy-start(f32[2,8]{1,0:T(2,128)} %get-tuple-element.208) | copy-start | bytes 196
  195.5 2.3 copy-start.2
  195.5 2.3 copy-start.15
  204.7 1.4 copy-start
  204.7 1.4 copy-start.21
Sparse Core Ops, SparseCore 0:
  37.8 79.3 all-gather.4
  119.1 123.8 all-gather.8
  244.8 119.2 all-gather.6
where the time goes:
time: 394 us; the launch traced here: 390 us
  waiting for transfers between devices  179 us (45%)
  other arithmetic  81.8 us (21%)
  local copies, waits for them, and re-layouts  53 us (13%)
  matrix products  34.2 us (9%)
  blocking collectives  25.1 us (6%)
  between operations  13.6 us (3%)
    all_gather x1, waiting for transfers between devices, local(): wide_all = lax.all_gather(normed, 'head', axis=1, tiled=True)  121 us
    select_n x62, other arithmetic, step(): jnp.where(position < mine, new, old)  57.5 us
    all_gather x1, waiting for transfers between devices, local(): full_weight = lax.all_gather(out_weight, ('dp', 'seq'), axis=0, tiled=True)  34.6 us
    all_gather x1, blocking collectives, entering(): pieces = jax.tree.map(lambda part: lax.all_gather(part, axis), value)  25.1 us
    all_gather x1, waiting for transfers between devices, entering(): pieces = jax.tree.map(lambda part: lax.all_gather(part, axis), value)  22.5 us
    mul x31, local copies, waits for them, and re-layouts, combine_states(): second_pair[0][..., None, None] * first_pair[1] + second_pair[1]  20.5 us
    dot_general x1, matrix products, local(): jnp.dot(wide_all, full_weight, preferred_element_type=jnp.float32)  19.8 us
  transfers between devices with their start and end apart: 4, of which 3 were waited for; matrix products, arithmetic and copies ran while one was open for 33% of the time, Pallas kernels for 0%

commit v1 on v0

--- a/solution.py
+++ b/solution.py
@@ -153,7 +153,9 @@
         * norm_gain.reshape(group_count, per_group * HEAD_SIZE)
     )
     normed = normed.astype(jnp.bfloat16).reshape(roll_count * tok_count, wide_x)
-    wide_all = lax.all_gather(normed, "head", axis=1, tiled=True)
+    wide_all = jnp.concatenate(
+        lax.all_to_all(jnp.stack([normed] * lax.axis_size("head")), "head", 0, 0), axis=1
+    )
     full_weight = lax.all_gather(out_weight, ("dp", "seq"), axis=0, tiled=True)
     mixed_terms = jnp.dot(wide_all, full_weight, preferred_element_type=jnp.float32)
     return mixed_terms.astype(jnp.bfloat16).reshape(roll_count, tok_count, -1)

time: 394 us -> 404 us (1.025)
  waiting for transfers between devices: 179 us -> 168 us
  local copies, waits for them, and re-layouts: 53 us -> 62.6 us
  starting transfers between devices: 3.75 us -> 10.6 us
    all_gather x1 -> x0, waiting for transfers between devices: 121 us -> none  [local(): wide_all = lax.all_gather(normed, 'head', axis=1, tiled=True)]
    all_to_all x0 -> x1, waiting for transfers between devices: none -> 90.1 us  [local(): lax.all_to_all(jnp.stack([normed] * lax.axis_size('head')), 'head', 0, 0)]
    all_gather x1, waiting for transfers between devices: 34.6 us -> 54.7 us  [local(): full_weight = lax.all_gather(out_weight, ('dp', 'seq'), axis=0, tiled=True)]
    all_to_all x0 -> x1, starting transfers between devices: none -> 6.88 us  [local(): lax.all_to_all(jnp.stack([normed] * lax.axis_size('head')), 'head', 0, 0)]
    reshape x1 -> x2, local copies, waits for them, and re-layouts: 0.01 us -> 6.18 us  [the longest x1 6.17 us: local(): (intra_out + inter_out + skip_shaped * x_shaped.astype(jnp.float32)).resh...]
  transfers between devices with their start and end apart: 4 -> 4, of which waited for: 3 -> 3; matrix products, arithmetic and copies ran while one was open for 33% -> 36% of each run, Pallas kernels for 0% -> 0%
where the time goes in v1:
time: 404 us; the launch traced here: 397 us
  waiting for transfers between devices  168 us (42%)
  other arithmetic  82.5 us (20%)
  local copies, waits for them, and re-layouts  62.6 us (15%)
  matrix products  34.2 us (8%)
  blocking collectives  25 us (6%)
  between operations  13.8 us (3%)
  starting transfers between devices  10.6 us (3%)
    all_to_all x1, waiting for transfers between devices, local(): lax.all_to_all(jnp.stack([normed] * lax.axis_size('head')), 'head', 0, 0)  90.1 us
    select_n x62, other arithmetic, step(): jnp.where(position < mine, new, old)  57.3 us
    all_gather x1, waiting for transfers between devices, local(): full_weight = lax.all_gather(out_weight, ('dp', 'seq'), axis=0, tiled=True)  54.7 us
    all_gather x1, blocking collectives, entering(): pieces = jax.tree.map(lambda part: lax.all_gather(part, axis), value)  25 us
    all_gather x1, waiting for transfers between devices, entering(): pieces = jax.tree.map(lambda part: lax.all_gather(part, axis), value)  22.7 us
    mul x31, local copies, waits for them, and re-layouts, combine_states(): second_pair[0][..., None, None] * first_pair[1] + second_pair[1]  20.5 us
    dot_general x1, matrix products, local(): jnp.dot(wide_all, full_weight, preferred_element_type=jnp.float32)  19.8 us
  transfers between devices with their start and end apart: 4, of which 3 were waited for; matrix products, arithmetic and copies ran while one was open for 36% of the time, Pallas kernels for 0%

profile of v1, /device:TPU:65, one launch (start us, length us, event | category | flops | bytes accessed | tf_op | source)
XLA Modules:
  0.0 397.1 jit_solution(3130618944018072615)
XLA Ops:
  9.6 3.7 collective-permute-start
  14.9 3.4 reduce-window.6
  22.3 1.7 copy.154
  26.2 3.5 multiply_convert_fusion.3
  29.7 2.1 reshape.550
  33.5 2.6 multiply_convert_fusion.2
  38.9 2.6 copy.182
  41.5 3.9 convert_multiply_fusion
  45.4 5.9 %reshape.564 = f32[1,3,256,2,8,64]{2,1,5,4,3,0:T(4,128)} reshape(f32[1,768,1024]{1,2,0:T(8,128)} %convert_multiply_fusion) | data formatting | bytes 6291456 | tf_op jit(solution)/shard_map/reshape | solution.py:145
  52.0 25.0 %all-gather = f32[32,2,8,1]{2,1,3,0:T(2,128)} all-gather(f32[1,2,8,1]{2,1,3,0:T(2,128)S(1)} %copy-done.18), channel_id=2, replica_groups=mesh['dp'=2,'seq'=32,'head'=4] {'seq'}, dimensions={0}, use_global_device_ids=true | all-gather | bytes 2112 | tf_op jit(solution)/shard_map/all_gather | solution.py:21
  78.4 5.7 %reshape.568 = f32[1,3,256,2,8,64]{2,1,5,4,3,0:T(4,128)} reshape(bf16[1,768,1024]{1,2,0:T(8,128)(2,1)} %copy-done.1) | data formatting | bytes 4718592 | tf_op jit(solution)/shard_map/convert_element_type | solution.py:108
  84.3 1.2 multiply_convert_fusion.5
  85.6 1.5 fusion.44
  87.1 7.5 %fusion.1 = f32[3,2,8,64,256]{4,3,2,1,0:T(8,128)} fusion(f32[2,3,256,256]{3,2,0,1:T(8,128)} %fusion.44, pred[256,256]{1,0:T(8,128)(4,1)S(1)} %iota_compare_fusion, bf16[3,256,2,8,64]{1,0,4,3,2:T(4,128)(2,1)} %reshape.550, f32[2,8,3,256]{3,1,2,0:T(8,128)S(1)} %bitcast.157, f32[2,8,3,256]{3,1,2,0:T(8,128)S(1)} %copy-done.8), kind=kOutput, calls=%fused_computation.5 | convolution fusion | flops 421527552 | bytes 6455296 | tf_op jit(solution)/shard_map/rgkcqs,rcsgkp->rcqgkp/dot_general | solution.py:102
  94.6 22.7 %all-gather.4.cloned.1.call-done = f32[32,1,2,8,64,128]{5,4,3,2,1,0:T(8,128)} async-done(((f32[1,1,2,8,64,128]{5,4,3,2,1,0:T(8,128)}), f32[32,1,2,8,64,128]{5,4,3,2,1,0:T(8,128)}) %all-gather.4.cloned.1.call-update) | async-done | bytes 16777232 | tf_op jit(solution)/shard_map/all_gather | solution.py:21
  117.4 78.0 %while.16 = (s32[]{:T(128)}, f32[1,2,8]{2,1,0:T(2,128)S(1)}, f32[1,2,8,64,128]{4,3,2,1,0:T(8,128)S(1)}, s32[]{:T(128)}, f32[32,1,2,8]{3,2,1,0:T(2,128)}, /*index...) while((s32[]{:T(128)}, f32[1,2,8]{2,1,0:T(2,128)S(1)}, ...), condition=%wide.region_3.4_spmd.clone, body=%wide.region_2.3_spmd.clone.sunk | while | flops 524340 | bytes 1573367 | solution.py:30
  118.1 1.2 fusion.59
  120.6 1.2 fusion.59
  123.1 1.2 fusion.59
  125.6 1.2 fusion.59
  138.0 1.2 fusion.59
  143.0 1.2 fusion.59
  145.6 1.2 fusion.59
  150.6 1.2 fusion.59
  153.2 1.2 fusion.59
  155.7 1.2 fusion.59
  158.3 1.2 fusion.59
  160.8 1.2 fusion.59
  163.4 1.2 fusion.59
  173.4 1.2 fusion.59
  175.9 1.2 fusion.59
  178.4 1.2 fusion.59
  180.9 1.2 fusion.59
  183.4 1.2 fusion.59
  186.0 1.2 fusion.59
  188.5 1.2 fusion.59
  191.0 1.2 fusion.59
  193.5 1.2 fusion.59
  195.7 1.8 copy-done.2
  197.6 4.8 %fusion.19 = (f32[3,256,2]{1,2,0:T(2,128)S(1)}, f32[1,3,256,2,8,64]{2,5,4,3,1,0:T(8,128)S(1)}) fusion(f32[1,3,256,2,8,64]{2,1,5,4,3,0:T(4,128)S(1)} %copy-done.2, f32[1,3,256,2,8,64]{2,1,5,4,3,0:T(4,128)} %reshape.568, f32[2,8]{1,0:T(2,128)S(1)} %copy-done.15, f32[3,256,2,8]{1,3,2,0:T(8,128)S(1)} %bitcast.159, ...), kind=kOutput, calls=%fused_computation.34 | convolution fusion | flops 1214249472 | bytes 14604352 | tf_op jit(solution)/shard_map/rcqgn,rgkcpn->rcqgkp/dot_general | solution.py:139
  202.4 4.1 %copy.181 = f32[1,3,256,2,8,64]{2,1,5,4,3,0:T(4,128)} copy(f32[1,3,256,2,8,64]{2,5,4,3,1,0:T(8,128)S(1)} %get-tuple-element.215) | data formatting | bytes 6291456 | tf_op jit(solution)/shard_map/add | solution.py:142
  206.5 6.2 %reshape.563 = f32[1,768,1024]{1,2,0:T(8,128)} reshape(f32[1,3,256,2,8,64]{2,1,5,4,3,0:T(4,128)} %copy.181) | data formatting | bytes 6291456 | tf_op jit(solution)/shard_map/reshape | solution.py:142
  212.7 3.0 fusion.17
  215.8 3.0 stack.19
  218.8 6.9 %all-to-all-start = ((bf16[4,768,1024]{1,2,0:T(8,128)(2,1)}), bf16[4,768,1024]{1,2,0:T(8,128)(2,1)}, u32[]{:S(2)}, u32[]{:S(2)}) async-start(bf16[4,768,1024]{1,2,0:T(8,128)(2,1)} %stack.19), calls=%async_computation | async-start | bytes 12582912 | tf_op jit(solution)/shard_map/all_to_all | solution.py:157
  225.7 54.7 %all-gather.6.cloned.1.call-done = bf16[4096,2048]{1,0:T(8,128)(2,1)} async-done(((bf16[64,2048]{1,0:T(8,128)(2,1)}), bf16[4096,2048]{1,0:T(8,128)(2,1)}) %all-gather.6.cloned.1.call-update) | async-done | bytes 16777232 | tf_op jit(solution)/shard_map/all_gather | solution.py:159
  280.4 90.1 %all-to-all-done = bf16[4,768,1024]{1,2,0:T(8,128)(2,1)} async-done(((bf16[4,768,1024]{1,2,0:T(8,128)(2,1)}), bf16[4,768,1024]{1,2,0:T(8,128)(2,1)}, u32[]{:S(2)}, u32[]{:S(2)}) %all-to-all-start) | async-done | bytes 6291488 | tf_op jit(solution)/shard_map/all_to_all | solution.py:157
  370.4 19.8 %fusion.20 = bf16[1,768,2048]{2,1,0:T(8,128)(2,1)} fusion(bf16[768,4096]{0,1:T(8,128)(2,1)} %bitcast.54, bf16[4096,2048]{1,0:T(8,128)(2,1)} %all-gather.6.cloned.1.call-done), kind=kOutput, calls=%fused_computation.37 | convolution fusion | flops 12886474752 | bytes 26214400 | tf_op jit(solution)/shard_map/dot_general | solution.py:160
  (171 shorter events, 69.6 us)
Async XLA Ops:
  6.5 110.8 %all-gather.4.cloned.1.call-start = ((), (), s32[]{:S(2)}) async-start(), calls=%async_computation.1 | async-start | bytes 17301504 | tf_op jit(solution)/shard_map/all_gather | solution.py:21
  9.6 14.8 %collective-permute-start = (bf16[1,3,1536]{1,2,0:T(8,128)(2,1)}, bf16[1,3,1536]{1,2,0:T(8,128)(2,1)}, u32[]{:S(2)}, u32[]{:S(2)}) collective-permute-start(bf16[1,3,1536]{1,2,0:T(8,128)(2,1)} %copy.153), channel_id=1, source_target_pairs={{0,4},{4,8},{8,12},{12,16},{16,20},{20,24},{24,28},{28,32},{32,36}... | collective-permute-start | bytes 27656 | tf_op jit(solution)/shard_map/ppermute | solution.py:16
  14.8 5.7 %copy-start.12 = (f32[4,1024]{1,0:T(4,128)S(1)}, f32[4,1024]{1,0:T(4,128)}, u32[]{:S(2)}) copy-start(f32[4,1024]{1,0:T(4,128)} %param.23) | copy-start | bytes 49156
  14.8 5.7 %copy-start.19 = (f32[4,256]{1,0:T(4,128)S(1)}, f32[4,256]{1,0:T(4,128)}, u32[]{:S(2)}) copy-start(f32[4,256]{1,0:T(4,128)} %param.24) | copy-start | bytes 12292
  18.6 3.1 copy-start.6
  21.1 15.6 %copy-start.13 = (f32[2,8]{1,0:T(2,128)}, f32[2,8]{1,0:T(2,128)S(1)}, u32[]{:S(2)}) copy-start(f32[2,8]{1,0:T(2,128)S(1)} %get-tuple-element.212) | copy-start | bytes 196
  22.3 14.4 %copy-start.10 = (f32[2,8]{1,0:T(2,128)}, f32[2,8]{1,0:T(2,128)S(1)}, u32[]{:S(2)}) copy-start(f32[2,8]{1,0:T(2,128)S(1)} %get-tuple-element.209) | copy-start | bytes 196
  29.7 3.7 copy-start.1
  29.7 3.1 copy-start.4
  37.7 242.6 %all-gather.6.cloned.1.call-start = ((), (), s32[]{:S(2)}) async-start(), calls=%async_computation.2 | async-start | bytes 17039360 | tf_op jit(solution)/shard_map/all_gather | solution.py:159
  45.4 5.9 %copy-start.22 = (f32[16]{0:T(128)S(1)}, f32[16]{0:T(128)}, u32[]{:S(2)}) copy-start(f32[16]{0:T(128)} %param.21) | copy-start | bytes 196
  45.4 6.6 %copy-start.18 = (f32[1,2,8,1]{2,1,3,0:T(2,128)S(1)}, f32[1,2,8,1]{2,1,3,0:T(2,128)}, u32[]{:S(2)}) copy-start(f32[1,2,8,1]{2,1,3,0:T(2,128)} %get-tuple-element.211) | copy-start | bytes 196
  45.4 31.6 %copy-start.20 = (f32[4,256]{1,0:T(4,128)S(1)}, f32[4,256]{1,0:T(4,128)}, u32[]{:S(2)}) copy-start(f32[4,256]{1,0:T(4,128)} %param.25) | copy-start | bytes 12292
  45.4 32.3 %copy-start.7 = (f32[2,8,3,2]{1,3,2,0:T(2,128)S(1)}, f32[2,8,3,2]{1,3,2,0:T(2,128)}, u32[]{:S(2)}) copy-start(f32[2,8,3,2]{1,3,2,0:T(2,128)} %copy-done.6) | copy-start | bytes 1156
  51.4 32.8 %copy-start.5 = (bf16[1,768,256]{2,1,0:T(8,128)(2,1)S(1)}, bf16[1,768,256]{2,1,0:T(8,128)(2,1)}, u32[]{:S(2)}) copy-start(bf16[1,768,256]{2,1,0:T(8,128)(2,1)} %param.17) | copy-start | bytes 1179652
  84.3 2.9 copy-start.8
  87.1 30.2 %copy-start.9 = (f32[1,2,8]{2,1,0:T(2,128)S(1)}, f32[1,2,8]{2,1,0:T(2,128)}, u32[]{:S(2)}) copy-start(f32[1,2,8]{2,1,0:T(2,128)} %custom-call) | copy-start | bytes 196
  117.3 78.0 %copy-start.3 = (f32[1,16,64,128]{3,2,1,0:T(8,128)S(1)}, f32[1,16,64,128]{3,2,1,0:T(8,128)}, u32[]{:S(2)}) copy-start(f32[1,16,64,128]{3,2,1,0:T(8,128)} %param.26) | copy-start | bytes 1572868
  117.3 78.0 %copy-start.11 = (f32[2,8]{1,0:T(2,128)S(1)}, f32[2,8]{1,0:T(2,128)}, u32[]{:S(2)}) copy-start(f32[2,8]{1,0:T(2,128)} %copy-done.10) | copy-start | bytes 196
  117.3 78.0 %copy-start.16 = (f32[2,8]{1,0:T(2,128)S(1)}, f32[2,8]{1,0:T(2,128)}, u32[]{:S(2)}) copy-start(f32[2,8]{1,0:T(2,128)} %get-tuple-element.213) | copy-start | bytes 196
  117.4 78.2 %copy-start.14 = (f32[2,8]{1,0:T(2,128)S(1)}, f32[2,8]{1,0:T(2,128)}, u32[]{:S(2)}) copy-start(f32[2,8]{1,0:T(2,128)} %copy-done.13) | copy-start | bytes 196
  117.4 78.2 %copy-start.17 = (f32[2,8]{1,0:T(2,128)S(1)}, f32[2,8]{1,0:T(2,128)}, u32[]{:S(2)}) copy-start(f32[2,8]{1,0:T(2,128)} %get-tuple-element.208) | copy-start | bytes 196
  195.3 2.3 copy-start.2
  195.3 2.3 copy-start.15
  206.5 6.2 %copy-start = (bf16[1,768,1024]{1,2,0:T(8,128)(2,1)S(1)}, bf16[1,768,1024]{1,2,0:T(8,128)(2,1)}, u32[]{:S(2)}) copy-start(bf16[1,768,1024]{1,2,0:T(8,128)(2,1)} %copy.182) | copy-start | bytes 4718596
  206.5 6.2 %copy-start.21 = (f32[1024]{0:T(1024)S(1)}, f32[1024]{0:T(1024)}, u32[]{:S(2)}) copy-start(f32[1024]{0:T(1024)} %param.22) | copy-start | bytes 12292
  218.8 151.6 %all-to-all-start = ((bf16[4,768,1024]{1,2,0:T(8,128)(2,1)}), bf16[4,768,1024]{1,2,0:T(8,128)(2,1)}, u32[]{:S(2)}, u32[]{:S(2)}) async-start(bf16[4,768,1024]{1,2,0:T(8,128)(2,1)} %stack.19), calls=%async_computation | async-start | bytes 12582912 | tf_op jit(solution)/shard_map/all_to_all | solution.py:157
Sparse Core Ops, SparseCore 0:
  37.8 79.4 all-gather.3
  119.2 161.1 all-gather.5
